TPU v7x, 32 devices: a whole 2x2x4 slice. The times are simulated.
32 devices in a mesh: gx: 8 (over z, core), gy: 4 (over y, x).
Axes of the slice: x: 2, y: 2, z: 4, core: 2. Of those that a mesh axis runs over, the one named last changes fastest.
Arguments:
- rhs: float32 [64, 32, 6, 3, 256], P('gx', 'gy'), may hold values from -400 to 400
- contrast: float32 [64, 32, 256], P('gx', 'gy'), may hold values from 0.2 to 2
- occupied: int32 [64, 32], P('gx', 'gy'), may hold values 0 or 1
- near: bfloat16 [5, 768, 768], replicated, may hold values from -0.078125 to 0.078125
- basis: bfloat16 [768, 64], replicated, may hold values from -0.21875 to 0.21875
- transfer: float32 [4, 4, 64, 64], replicated, may hold values from -0.5 to 0.5
- coupling: float32 [5, 20, 64, 64], replicated, may hold values from -0.15625 to 0.15625
Outputs:
- third: float32 [64, 32, 6, 3, 256], P('gx', 'gy')
- hess: float32 [6, 6], replicated
All inputs are finite; a program needn't handle non-finite values. No bound on the sum of `occupied` on one device may be relied on, other than what follows from the above.
Results may differ from a plain program's by a relative error of at most 0.0031.
Values may be sent and summed in bfloat16 or wider, within the bound.
A program may use at most 128 MiB of HBM per device.

v0:
```python
import functools

import jax
import jax.numpy as jnp
from jax import lax
from jax.experimental import pallas as pl
from jax.experimental.pallas import tpu as pltpu
from jax.sharding import PartitionSpec as P

EPSILON = 1e-06
NEAR_BASE = ((0, 0), (1, -1), (1, 0), (1, 1), (0, 1))
AROUND = [(a, b) for a in (-1, 0, 1) for b in (-1, 0, 1)]
COMPASS = [d for d in AROUND if d != (0, 0)]
MESH = pl.DeviceIdType.MESH
VMEM = pl.BlockSpec(memory_space=pltpu.VMEM)


def near_lookup():
    table = {}
    for slot, (a, b) in enumerate(NEAR_BASE):
        table[(a, b)] = (slot, False)
        if (a, b) != (0, 0):
            table[(-a, -b)] = (slot, True)
    return table


def far_lookup():
    base = [
        (a, b)
        for a in range(-3, 4)
        for b in range(-3, 4)
        if max(abs(a), abs(b)) >= 2 and (a > 0 or (a == 0 and b > 0))
    ]
    table = {}
    for slot, (a, b) in enumerate(base):
        table[(a, b)] = (slot, False)
        table[(-a, -b)] = (slot, True)
    return table


def halves(values):
    high = values.astype(jnp.bfloat16)
    return high, (values - high.astype(jnp.float32)).astype(jnp.bfloat16)


def far_level(depth, coupling, high, low):
    table = far_lookup()
    rank = coupling.shape[2]
    children = [(c, e) for c in (0, 1) for e in (0, 1)]
    empty = jnp.zeros((rank, rank), jnp.float32)
    row = 0
    for px, py in AROUND:
        for c, e in children:
            line = []
            for tc, te in children:
                found = table.get((2 * px + c - tc, 2 * py + e - te))
                if found is None:
                    line.append(empty)
                else:
                    block = coupling[depth, found[0]]
                    line.append(block.T if found[1] else block)
            high[depth, row : row + rank, :], low[depth, row : row + rank, :] = halves(
                jnp.concatenate(line, axis=1)
            )
            row += rank


def place(index, size_y):
    return {"gx": index // size_y, "gy": index % size_y}


def greet_all(size_x, size_y):
    total = size_x * size_y
    me = lax.axis_index("gx") * size_y + lax.axis_index("gy")
    barrier = pltpu.get_barrier_semaphore()

    def greet(step, carry):
        other = (me + step) % total
        pl.semaphore_signal(
            barrier, inc=1, device_id=place(other, size_y), device_id_type=MESH
        )
        return carry

    lax.fori_loop(1, total, greet, 0)


def await_greetings(size_x, size_y):
    pl.semaphore_wait(pltpu.get_barrier_semaphore(), size_x * size_y - 1)


def gather_copy(source, target, send, receive, step, size_x, size_y):
    total = size_x * size_y
    me = lax.axis_index("gx") * size_y + lax.axis_index("gy")
    other = (me + step) % total
    return pltpu.make_async_remote_copy(
        src_ref=source,
        dst_ref=target.at[me],
        send_sem=send.at[step],
        recv_sem=receive.at[step],
        device_id=place(other, size_y),
        device_id_type=MESH,
    )


def strip(move, length):
    if move > 0:
        return pl.ds(length, 1), pl.ds(0, 1)
    if move < 0:
        return pl.ds(1, 1), pl.ds(length + 1, 1)
    return pl.ds(1, length), pl.ds(1, length)


def stacked(values):
    high = values.astype(jnp.bfloat16).astype(jnp.float32)
    return jnp.concatenate([high, values - high], axis=0).astype(jnp.bfloat16)


def product(left, right, across=1):
    return lax.dot_general(
        left, right, (((1,), (1 - across,)), ((), ())), preferred_element_type=jnp.float32
    )


def times(values, high, low, across=1):
    both = stacked(values)
    total = product(both, high, across) + product(both, low, across)
    rows = values.shape[0]
    return total[:rows] + total[rows:]


def group(boxes, size_x, size_y):
    rows = []
    for x in range(0, size_x, 2):
        for y in range(0, size_y, 2):
            four = [(x + c) * size_y + y + e for c in (0, 1) for e in (0, 1)]
            rows.append(jnp.concatenate([boxes[8 * i : 8 * i + 8] for i in four], axis=1))
    return rows


def ungroup(parents, size_x, size_y):
    rank = parents.shape[1] // 4
    rows = []
    for x in range(2 * size_x):
        for y in range(2 * size_y):
            i = (x // 2) * size_y + y // 2
            k = 2 * (x % 2) + y % 2
            rows.append(parents[8 * i : 8 * i + 8, k * rank : (k + 1) * rank])
    return jnp.concatenate(rows, axis=0)


def clear_rim(out):
    long_x, long_y = out.shape[0], out.shape[1]
    line_x = jnp.zeros((1,) + out.shape[1:], out.dtype)
    line_y = jnp.zeros((long_x, 1) + out.shape[2:], out.dtype)
    out[0:1] = line_x
    out[long_x - 1 : long_x] = line_x
    out[:, 0:1] = line_y
    out[:, long_y - 1 : long_y] = line_y


def krylov_kernel(size_x, size_y, inner, count, *refs):
    rhs, weight, near_far_away, basis, lifts, coupling, third, hess = refs[:8]
    near, far_high, far_low, first, second, source = refs[8:14]
    padded = refs[14]
    pyramid = refs[15 : 15 + inner]
    rest = refs[15 + inner :]
    coarse = coupling.shape[0] - inner
    tops = rest[:coarse]
    mine, gathered, shifted, total, parts, slots = rest[coarse : coarse + 6]
    send, receive, gather_send, gather_receive, sum_send, sum_receive, load = rest[coarse + 6 :]
    side = source.shape[0]
    width = source.shape[3]
    rank = basis.shape[0]
    devices = size_x * size_y
    me_x, me_y = lax.axis_index("gx"), lax.axis_index("gy")
    me = me_x * size_y + me_y
    ways = range(len(COMPASS))
    bands = (padded,) + tuple(pyramid)
    rows = side * side * 8
    lane = lax.broadcasted_iota(jnp.int32, (8, 128), 1)

    def tile_of(columns):
        tile = jnp.zeros((8, 128), jnp.float32)
        for i, column in enumerate(columns):
            tile = jnp.where(lane == i, column, tile)
        return tile

    def start_sums(number, sums):
        tile = tile_of([jnp.sum(value, axis=1, keepdims=True) for value in sums])
        parts[number] = tile
        slots[number, me] = tile

        def begin(step, carry):
            gather_copy(
                parts.at[number],
                slots.at[number],
                sum_send.at[number],
                sum_receive.at[number],
                step,
                size_x,
                size_y,
            ).start()
            return carry

        lax.fori_loop(1, devices, begin, 0)

    def finish_gather(piece, target, sent, received):
        def finish(step, carry):
            other = (me + devices - step) % devices
            pltpu.make_async_remote_copy(
                src_ref=piece,
                dst_ref=target.at[other],
                send_sem=sent.at[step],
                recv_sem=received.at[step],
                device_id=place((me + step) % devices, size_y),
                device_id_type=MESH,
            ).wait()
            return carry

        lax.fori_loop(1, devices, finish, 0)

    def finish_sums(number, amount):
        finish_gather(
            parts.at[number], slots.at[number], sum_send.at[number], sum_receive.at[number]
        )
        tile = jnp.sum(slots[number], axis=0) / count
        return [tile[:, i : i + 1] for i in range(amount)]

    def rows_sum(value):
        return jnp.sum(value, axis=0)

    def sweep(amount, work):
        def one(x, sums):
            return tuple(old + new for old, new in zip(sums, work(x)))

        return lax.fori_loop(0, side, one, (jnp.zeros((8, width), jnp.float32),) * amount)

    near_copy = pltpu.make_async_copy(near_far_away, near, load.at[0])
    near_copy.start()
    for band in bands + tuple(tops):
        clear_rim(band)
    greet_all(size_x, size_y)

    def rhs_sums(x):
        pieces = [jnp.swapaxes(rhs[x, :, part], 0, 1) for part in range(rhs.shape[2])]
        value = jnp.concatenate(pieces, axis=-1)
        blank = jnp.zeros((side, 8 - rhs.shape[1], width), jnp.float32)
        value = jnp.concatenate([value, blank], axis=1)
        first[x] = value
        return (rows_sum(value * value),)

    sums = sweep(1, rhs_sums)
    await_greetings(size_x, size_y)
    start_sums(0, sums)

    def build(depth, carry):
        far_level(depth, coupling, far_high, far_low)
        return carry

    lax.fori_loop(0, coupling.shape[0], build, 0)
    (square,) = finish_sums(0, 1)
    beta = jnp.sqrt(square + EPSILON)

    def copy_of(number, way):
        move_x, move_y = COMPASS[way]
        band = bands[number]
        from_x, to_x = strip(move_x, band.shape[0] - 2)
        from_y, to_y = strip(move_y, band.shape[1] - 2)
        return pltpu.make_async_remote_copy(
            src_ref=band.at[from_x, from_y],
            dst_ref=band.at[to_x, to_y],
            send_sem=send.at[number, way],
            recv_sem=receive.at[number, way],
            device_id={"gx": me_x + move_x, "gy": me_y + move_y},
            device_id_type=MESH,
        )

    def inside(place_x, place_y):
        return (place_x >= 0) & (place_x < size_x) & (place_y >= 0) & (place_y < size_y)

    def start_bands(numbers):
        for way in ways:
            move_x, move_y = COMPASS[way]

            @pl.when(inside(me_x + move_x, me_y + move_y))
            def _(way=way):
                for number in numbers:
                    copy_of(number, way).start()

    def finish_bands(numbers):
        for way in ways:
            move_x, move_y = COMPASS[way]

            @pl.when(inside(me_x + move_x, me_y + move_y))
            def _(way=way):
                for number in numbers:
                    copy_of(number, way).wait_send()

            @pl.when(inside(me_x - move_x, me_y - move_y))
            def _(way=way):
                for number in numbers:
                    copy_of(number, way).wait_recv()

    def operate():
        padded[1 : 1 + side, 1 : 1 + side] = source[...]
        start_bands((0,))

        flat = source[...].astype(jnp.float32).reshape(side * side * 8, width).astype(jnp.bfloat16)
        level = product(flat, basis[...], 0)
        span = side
        for depth in range(inner):
            parents = group(level, span, span)
            span //= 2
            for i, parent in enumerate(parents):
                pyramid[depth][1 + i // span, 1 + i % span] = parent
            high, low = halves(lifts[depth])
            level = times(jnp.concatenate(parents, axis=0), high, low)
        mine[...] = level
        gathered[me] = level
        start_bands(range(1, inner + 1))

        def begin(step, carry):
            gather_copy(mine, gathered, gather_send, gather_receive, step, size_x, size_y).start()
            return carry

        lax.fori_loop(1, devices, begin, 0)

        box_row = side * 8
        shifted[1, box_row : box_row + rows] = flat
        table = near_lookup()
        chunk = 256 if width % 256 == 0 else 128

        def near_term(a, b, columns, begin, end):
            slot, flipped = table[(a, b)]
            piece = shifted[1 + b, begin * box_row : end * box_row]
            if flipped:
                return product(piece, near[slot, columns, :], 0)
            return product(piece, near[slot, :, columns])

        def own_columns(index, carry):
            columns = pl.ds(pl.multiple_of(index * chunk, chunk), chunk)
            total[:, columns] = near_term(0, 0, columns, 1, side + 1)
            total[: rows - box_row, columns] += near_term(1, 0, columns, 2, side + 1)
            total[box_row:, columns] += near_term(-1, 0, columns, 1, side)
            return carry

        lax.fori_loop(0, width // chunk, own_columns, 0)
        finish_bands((0,))
        for b in (0, 2):
            shifted[b] = (
                padded[:, b : b + side]
                .astype(jnp.float32)
                .reshape((side + 2) * side * 8, width)
                .astype(jnp.bfloat16)
            )
        for x in (0, side + 1):
            shifted[1, x * box_row : (x + 1) * box_row] = (
                padded[x, 1 : 1 + side]
                .astype(jnp.float32)
                .reshape(box_row, width)
                .astype(jnp.bfloat16)
            )

        def near_columns(index, carry):
            columns = pl.ds(pl.multiple_of(index * chunk, chunk), chunk)
            value = total[:, columns]
            for a in (-1, 0, 1):
                for b in (-1, 1):
                    value = value + near_term(a, b, columns, 1 + a, 1 + a + side)
            total[:, columns] = value
            total[rows - box_row :, columns] += near_term(1, 0, columns, side + 1, side + 2)
            total[:box_row, columns] += near_term(-1, 0, columns, 0, 1)
            return carry

        lax.fori_loop(0, width // chunk, near_columns, 0)
        finish_bands(range(1, inner + 1))

        finish_gather(mine, gathered, gather_send, gather_receive)

        def couple(depth, window):
            value = None
            for k, (a, b) in enumerate(AROUND):
                span_rows = slice(4 * rank * k, 4 * rank * (k + 1))
                term = times(window(a, b), far_high[depth, span_rows], far_low[depth, span_rows])
                value = term if value is None else value + term
            return value

        across, along = size_x, size_y
        boxes = gathered[...].reshape(devices * 8, rank)
        for step in range(coarse):
            parents = group(boxes, across, along)
            across, along = across // 2, along // 2
            for i, parent in enumerate(parents):
                tops[step][1 + i // along, 1 + i % along] = parent
            if step < coarse - 1:
                high, low = halves(lifts[inner + step])
                boxes = times(jnp.concatenate(parents, axis=0), high, low)
        down = None
        for step in range(coarse - 1, -1, -1):
            near_x, near_y = me_x >> step + 1, me_y >> step + 1
            value = couple(
                inner + step, lambda a, b: tops[step][near_x + (1 + a), near_y + (1 + b)]
            )
            if down is not None:
                high, low = halves(lifts[inner + step])
                value = value + times(down, high, low, 0)
            child = 2 * (me_x >> step & 1) + (me_y >> step & 1)
            down = jnp.zeros((8, rank), jnp.float32)
            for i in range(4):
                down = jnp.where(child == i, value[:, i * rank : (i + 1) * rank], down)

        span = 1
        for depth in range(inner - 1, -1, -1):
            band = pyramid[depth]
            value = couple(
                depth,
                lambda a, b: band[1 + a : 1 + a + span, 1 + b : 1 + b + span].reshape(
                    span * span * 8, 4 * rank
                ),
            )
            high, low = halves(lifts[depth])
            value = value + times(down, high, low, 0)
            down = ungroup(value, span, span)
            span *= 2
        spread_down = product(stacked(down), basis[...])
        total[...] = total[...] + spread_down[:rows] + spread_down[rows:]

    boxes_of = side * 8

    def image_of(x, field):
        return field[x] + total[pl.ds(pl.multiple_of(x * boxes_of, 8), boxes_of)].reshape(
            side, 8, width
        )

    def wide_weight(x):
        return jnp.concatenate([weight[x]] * (width // weight.shape[3]), axis=-1)

    def set_first(x, carry):
        value = first[x] * inverse
        first[x] = value
        source[x] = (wide_weight(x) * value).astype(jnp.bfloat16)
        return carry

    inverse = 1.0 / beta
    lax.fori_loop(0, side, set_first, 0)
    near_copy.wait()
    operate()

    def first_sums(x):
        value, image = first[x], image_of(x, first)
        second[x] = image
        return rows_sum(value * image), rows_sum(image * image)

    start_sums(1, sweep(2, first_sums))
    h11, square = finish_sums(1, 2)
    h21 = jnp.sqrt(square - h11 * h11 + EPSILON)
    inverse_second = 1.0 / h21

    def set_second(x, carry):
        value = (second[x] - h11 * first[x]) * inverse_second
        second[x] = value
        source[x] = (wide_weight(x) * value).astype(jnp.bfloat16)
        return carry

    lax.fori_loop(0, side, set_second, 0)
    operate()

    def second_sums(x):
        image = image_of(x, second)
        third[x] = image
        return rows_sum(first[x] * image), rows_sum(second[x] * image), rows_sum(image * image)

    start_sums(2, sweep(3, second_sums))
    h12, h22, square = finish_sums(2, 3)
    h32 = jnp.sqrt(square - h12 * h12 - h22 * h22 + EPSILON)
    inverse_third = 1.0 / h32

    def set_third(x, carry):
        third[x] = (third[x] - h12 * first[x] - h22 * second[x]) * inverse_third
        return carry

    lax.fori_loop(0, side, set_third, 0)
    hess[...] = tile_of([beta, h11, h21, h12, h22, h32])


def krylov(rhs, weight, near, basis, lifts, coupling, count, size_x, size_y):
    side = rhs.shape[0]
    rank, width = basis.shape
    boxes = (side, side, 8, width)
    inner = side.bit_length() - 1
    levels = coupling.shape[0]
    coarse = levels - inner
    devices = size_x * size_y
    halos = inner + 1
    scratch = [
        pltpu.VMEM(near.shape, near.dtype),
        pltpu.VMEM((levels, 36 * rank, 4 * rank), jnp.bfloat16),
        pltpu.VMEM((levels, 36 * rank, 4 * rank), jnp.bfloat16),
        pltpu.VMEM(boxes, jnp.float32),
        pltpu.VMEM(boxes, jnp.float32),
        pltpu.VMEM(boxes, jnp.bfloat16),
        pltpu.VMEM((side + 2, side + 2, 8, width), jnp.bfloat16),
    ]
    for depth in range(inner):
        span = (side >> depth + 1) + 2
        scratch.append(pltpu.VMEM((span, span, 8, 4 * rank), jnp.float32))
    for step in range(coarse):
        grid = ((size_x >> step + 1) + 2, (size_y >> step + 1) + 2)
        scratch.append(pltpu.VMEM(grid + (8, 4 * rank), jnp.float32))
    scratch += [
        pltpu.VMEM((8, rank), jnp.float32),
        pltpu.VMEM((devices, 8, rank), jnp.float32),
        pltpu.VMEM((3, (side + 2) * side * 8, width), jnp.bfloat16),
        pltpu.VMEM((side * side * 8, width), jnp.float32),
        pltpu.VMEM((3, 8, 128), jnp.float32),
        pltpu.VMEM((3, devices, 8, 128), jnp.float32),
        pltpu.SemaphoreType.DMA((halos, len(COMPASS))),
        pltpu.SemaphoreType.DMA((halos, len(COMPASS))),
        pltpu.SemaphoreType.DMA((devices,)),
        pltpu.SemaphoreType.DMA((devices,)),
        pltpu.SemaphoreType.DMA((3, devices)),
        pltpu.SemaphoreType.DMA((3, devices)),
        pltpu.SemaphoreType.DMA((1,)),
    ]
    return pl.pallas_call(
        functools.partial(krylov_kernel, size_x, size_y, inner, count),
        in_specs=[VMEM, VMEM, pl.BlockSpec(memory_space=pl.ANY), VMEM, VMEM, VMEM],
        out_specs=[VMEM, VMEM],
        out_shape=[
            jax.ShapeDtypeStruct(boxes, jnp.float32),
            jax.ShapeDtypeStruct((8, 128), jnp.float32),
        ],
        scratch_shapes=scratch,
        compiler_params=pltpu.CompilerParams(collective_id=0, has_side_effects=True),
    )(rhs, weight, near, basis, lifts, coupling)


def body(rhs, contrast, occupied, near, basis, transfer, coupling):
    shape = rhs.shape
    side, _, fields, parts, voxels = shape
    width = parts * voxels
    rank = basis.shape[1]
    devices_x = lax.axis_size("gx")
    devices_y = lax.axis_size("gy")
    count = float(side * side * devices_x * devices_y * width)
    flat = rhs.transpose(0, 2, 3, 1, 4)
    weight = occupied.astype(jnp.float32)[:, :, None] * contrast
    weight = weight[:, :, None, :]
    lifts = transfer.reshape(transfer.shape[0], 4 * rank, rank)
    third, hess = krylov(
        flat, weight, near, basis.T, lifts, coupling, count, devices_x, devices_y
    )
    return (third[:, :, :fields].reshape(shape), hess[:fields, :6])


def solution(mesh):
    placed = (
        P("gx", "gy", None, None, None),
        P("gx", "gy", None),
        P("gx", "gy"),
        P(),
        P(),
        P(),
        P(),
    )
    return jax.shard_map(
        body,
        mesh=mesh,
        in_specs=placed,
        out_specs=(P("gx", "gy", None, None, None), P()),
        check_vma=False,
    )
```

profile of v0, /device:TPU:0, one launch (start us, length us, event | category | flops | bytes accessed | tf_op | source)
XLA Modules:
  0.0 77.4 jit_solution(1479013570174681702)
XLA Ops:
  0.6 0.7 convert_element_type.3
  1.3 0.9 %broadcast_multiply_fusion = f32[8,8,256]{2,1,0:T(8,128)S(1)} fusion(f32[8,8,256]{2,1,0:T(8,128)} %param.8, f32[8,8]{1,0:T(8,128)S(1)} %convert_element_type.3), kind=kLoop, calls=%fused_computation | loop fusion | flops 16384 | bytes 131328 | tf_op jit(solution)/shard_map/mul | solution.py:547
  2.2 0.7 broadcast_in_dim.4.refs_1_
  2.9 70.1 %shard_map.86 = (f32[8,8,8,768]{3,2,1,0:T(8,128)}, f32[8,128]{1,0:T(8,128)}) custom-call(f32[8,6,3,8,256]{4,3,2,1,0:T(8,128)} %bitcast.6, f32[8,8,1,256]{3,2,1,0:T(1,128)} %broadcast_in_dim.4.refs_1_, bf16[5,768,768]{2,1,0:T(8,128)(2,1)} %refs_2_.1, bf16[64,768]{1,0:T(8,128)(2,1)} %bitcast.8, f32[4,256,64]{2,1,0:T(8,128)} %bitcast.7, f32[5,20,64,64]{3,2,1,0:T(8,128)} %refs_5_.1), custom_call_target="tpu_custom_call" | custom-call | tf_op jit(solution)/shard_map/pallas_call | solution.py:525
  73.0 2.4 %reshape.13 = f32[8,8,6,3,256]{4,3,2,1,0:T(4,128)S(1)} reshape(f32[8,8,6,768]{3,2,1,0:T(8,128)} %bitcast.5) | data formatting | bytes 2359296 | tf_op jit(solution)/shard_map/reshape | solution.py:553
  75.4 0.0 copy-start
  75.4 1.4 %copy.11 = f32[8,8,6,3,256]{4,1,3,2,0:T(8,128)} copy(f32[8,8,6,3,256]{4,3,2,1,0:T(4,128)S(1)} %reshape.13) | data formatting | bytes 2359296
  76.8 0.0 copy-done
  76.8 0.6 copy.15
Async XLA Ops:
  75.4 1.4 %copy-start = (f32[8,128]{1,0:T(8,128)S(1)}, f32[8,128]{1,0:T(8,128)}, u32[]{:S(2)}) copy-start(f32[8,128]{1,0:T(8,128)} %get-tuple-element.5) | copy-start | bytes 12292
where the time goes:
time: 77.7 us; the launch traced here: 77.4 us
  Pallas kernels  70.1 us (90%)
  local copies, waits for them, and re-layouts  5.06 us (7%)
  other arithmetic  1.6 us (2%)
    pallas_call x1, Pallas kernels, krylov(): pl.pallas_call(functools.partial(krylov_kernel, size_x, size_y, inner, co...  70.1 us
    reshape x1, local copies, waits for them, and re-layouts, body(): return (third[:, :, :fields].reshape(shape), hess[:fields, :6])  2.42 us
    unnamed x4, local copies, waits for them, and re-layouts  1.97 us

commit v1 on v0

v1 whole, which is shorter than its diff:
```python
import functools

import jax
import jax.numpy as jnp
from jax import lax
from jax.experimental import pallas as pl
from jax.experimental.pallas import tpu as pltpu
from jax.sharding import PartitionSpec as P

EPSILON = 1e-06
SHRINK = 2.0**-20
NEAR_BASE = ((0, 0), (1, -1), (1, 0), (1, 1), (0, 1))
HALF_RING = NEAR_BASE[1:]
AROUND = [(a, b) for a in (-1, 0, 1) for b in (-1, 0, 1)]
COMPASS = [d for d in AROUND if d != (0, 0)]
CHILDREN = [(c, e) for c in (0, 1) for e in (0, 1)]
MESH = pl.DeviceIdType.MESH
F32 = jnp.float32
BF16 = jnp.bfloat16


def near_lookup():
    table = {}
    for slot, (a, b) in enumerate(NEAR_BASE):
        table[(a, b)] = (slot, False)
        if (a, b) != (0, 0):
            table[(-a, -b)] = (slot, True)
    return table


def far_lookup():
    base = [
        (a, b)
        for a in range(-3, 4)
        for b in range(-3, 4)
        if max(abs(a), abs(b)) >= 2 and (a > 0 or (a == 0 and b > 0))
    ]
    table = {}
    for slot, (a, b) in enumerate(base):
        table[(a, b)] = (slot, False)
        table[(-a, -b)] = (slot, True)
    return table


def halves(values):
    high = values.astype(BF16)
    return high, (values - high.astype(F32)).astype(BF16)


def far_level(depth, coupling, far):
    table = far_lookup()
    rank = coupling.shape[2]
    empty = jnp.zeros((rank, rank), F32)
    seen = {}

    def block_of(offset):
        if offset not in table:
            return empty
        if offset not in seen:
            slot, flipped = table[offset]
            block = coupling[depth, slot]
            seen[offset] = block.T if flipped else block
        return seen[offset]

    for i, (px, py) in enumerate(HALF_RING):
        for k, (c, e) in enumerate(CHILDREN):
            line = [block_of((2 * px + c - tc, 2 * py + e - te)) for tc, te in CHILDREN]
            high, low = halves(jnp.concatenate(line, axis=1))
            far[depth, i, 0, k * rank : (k + 1) * rank, :] = high
            far[depth, i, 1, k * rank : (k + 1) * rank, :] = low


def strip(move, length):
    if move > 0:
        return pl.ds(length, 1), pl.ds(0, 1)
    if move < 0:
        return pl.ds(1, 1), pl.ds(length + 1, 1)
    return pl.ds(1, length), pl.ds(1, length)


def stacked(values):
    high = values.astype(BF16).astype(F32)
    return jnp.concatenate([high, values - high], axis=0).astype(BF16)


def product(left, right, across=1):
    return lax.dot_general(
        left, right, (((1,), (1 - across,)), ((), ())), preferred_element_type=F32
    )


def times(values, high, low, across=1):
    both = stacked(values)
    total = product(both, high, across) + product(both, low, across)
    rows = values.shape[0]
    return total[:rows] + total[rows:]


def group(boxes, size_x, size_y):
    rows = []
    for x in range(0, size_x, 2):
        for y in range(0, size_y, 2):
            four = [(x + c) * size_y + y + e for c, e in CHILDREN]
            rows.append(jnp.concatenate([boxes[8 * i : 8 * i + 8] for i in four], axis=1))
    return rows


def child_of(parents, x, y, size_y):
    rank = parents.shape[1] // 4
    i = (x // 2) * size_y + y // 2
    k = 2 * (x % 2) + y % 2
    return parents[8 * i : 8 * i + 8, k * rank : (k + 1) * rank]


def ungroup(parents, size_x, size_y):
    return jnp.concatenate(
        [child_of(parents, x, y, size_y) for x in range(2 * size_x) for y in range(2 * size_y)],
        axis=0,
    )


def clear_rim(out):
    long_x, long_y = out.shape[0], out.shape[1]
    line_x = jnp.zeros((1,) + out.shape[1:], out.dtype)
    line_y = jnp.zeros((long_x, 1) + out.shape[2:], out.dtype)
    out[0:1] = line_x
    out[long_x - 1 : long_x] = line_x
    out[:, 0:1] = line_y
    out[:, long_y - 1 : long_y] = line_y


def fold(value):
    pieces = [value[:, i : i + 128] for i in range(0, value.shape[1], 128)]
    return functools.reduce(lambda a, b: a + b, pieces)


def krylov_kernel(size_x, size_y, inner, count, *refs):
    arguments, (third, hess), scratch = refs[:7], refs[7:9], refs[9:]
    rhs, contrast, occupied, near, basis, lifts, coupling = scratch[:7]
    far, lift_high, lift_low, basis_twice, weight, product_of, source = scratch[7:14]
    image, total, skeleton, edge_send, edge, corner, edge_wide, corner_wide = scratch[14:22]
    bands = scratch[22 : 22 + inner]
    rest = scratch[22 + inner :]
    levels = coupling.shape[0]
    coarse = levels - inner
    tops = rest[:coarse]
    mine, gathered, parts, slots = rest[coarse : coarse + 4]
    near_send, near_receive, band_send, band_receive = rest[coarse + 4 : coarse + 8]
    gather_send, gather_receive, sum_send, sum_receive, load, unload = rest[coarse + 8 :]

    side, fields, comps, _, voxels = rhs.shape
    rank, width = basis.shape
    slab = fields * side
    rows = side * slab
    devices = size_x * size_y
    me_x, me_y = lax.axis_index("gx"), lax.axis_index("gy")
    me = me_x * size_y + me_y
    chunk = 256 if width % 256 == 0 else 128
    lane = lax.broadcasted_iota(jnp.int32, (8, 128), 1)
    sublane = lax.broadcasted_iota(jnp.int32, (8, 128), 0)

    loads = [
        pltpu.make_async_copy(argument, here, load.at[i])
        for i, (argument, here) in enumerate(zip(arguments, scratch[:7]))
    ]
    for i in (0, 1, 2, 4, 5, 6, 3):
        loads[i].start()

    def wrap(value, size):
        return jnp.where(value >= size, value - size, value)

    def others(act):
        def line(shift_x):
            to_x, from_x = wrap(me_x + shift_x, size_x), wrap(me_x + size_x - shift_x, size_x)
            for shift_y in range(size_y):
                if not isinstance(shift_x, int) or (shift_x, shift_y) != (0, 0):
                    to_y = wrap(me_y + shift_y, size_y)
                    from_y = wrap(me_y + size_y - shift_y, size_y)
                    act(shift_x * size_y + shift_y, (to_x, to_y), from_x * size_y + from_y)

        if devices <= 64:
            for shift_x in range(size_x):
                line(shift_x)
        else:
            line(0)

            def one(shift_x, carry):
                line(shift_x)
                return carry

            lax.fori_loop(1, size_x, one, 0)

    for step in (0, 1):
        for side_rows in (slice(0, slab), slice((side + 1) * slab, (side + 2) * slab)):
            source[step, 1, side_rows] = jnp.zeros((slab, width), BF16)
        edge[step] = jnp.zeros(edge.shape[1:], BF16)
        corner[step] = jnp.zeros(corner.shape[1:], BF16)
        for band in bands:
            clear_rim(band.at[step])
    for top in tops:
        clear_rim(top)

    barrier = pltpu.get_barrier_semaphore()

    def greet(step, to, before):
        pl.semaphore_signal(
            barrier, inc=1, device_id={"gx": to[0], "gy": to[1]}, device_id_type=MESH
        )

    others(greet)

    def gather_copy(piece, target, sent, received, step, to, slot):
        return pltpu.make_async_remote_copy(
            src_ref=piece,
            dst_ref=target.at[slot],
            send_sem=sent.at[step],
            recv_sem=received.at[step],
            device_id={"gx": to[0], "gy": to[1]},
            device_id_type=MESH,
        )

    def start_gather(*what):
        others(lambda step, to, before: gather_copy(*what, step, to, me).start())

    def finish_gather(*what):
        others(lambda step, to, before: gather_copy(*what, step, to, before).wait())

    def sums_of(number):
        return parts.at[number], slots.at[number], sum_send.at[number], sum_receive.at[number]

    def put_sums(number, sums):
        tile = jnp.zeros((8, 128), F32)
        for i, of_fields in enumerate(sums):
            lines = [jnp.sum(value, axis=0, keepdims=True) for value in of_fields]
            lines.append(jnp.zeros((8 - fields, 128), F32))
            column = jnp.sum(jnp.concatenate(lines, axis=0), axis=1, keepdims=True)
            tile = tile + jnp.where(lane == 8 * i + sublane, column, 0.0)
        line = jnp.sum(tile, axis=0, keepdims=True)
        parts[number] = line
        slots[number, me] = line

    def finish_sums(number, amount):
        finish_gather(*sums_of(number))
        line = jnp.broadcast_to(jnp.sum(slots[number], axis=0) * (1.0 / count), (8, 128))
        return [
            jnp.sum(jnp.where(lane == 8 * i + sublane, line, 0.0), axis=1, keepdims=True)
            for i in range(amount)
        ]

    def spread(column):
        return [
            jnp.broadcast_to(column[field : field + 1, :], (8, voxels)) for field in range(fields)
        ]

    def sweep(amount, work):
        zero = tuple(jnp.zeros((8, 128), F32) for _ in range(amount * fields))

        def one(x, sums):
            sums = [list(sums[i * fields : (i + 1) * fields]) for i in range(amount)]

            def add(i, field, value):
                sums[i][field] = sums[i][field] + fold(value)

            work(x, add)
            return tuple(value for of_fields in sums for value in of_fields)

        out = lax.fori_loop(0, side, one, zero)
        return [out[i * fields : (i + 1) * fields] for i in range(amount)]

    def tiles(x):
        for field in range(fields):
            place = pl.ds(pl.multiple_of(x * slab + field * side, 8), side)
            for part in range(comps):
                yield field, part, place, slice(part * voxels, (part + 1) * voxels)

    def put_product(part, place, value):
        for i in range(voxels // 128):
            product_of[part * (voxels // 128) + i, place] = value[:, i * 128 : (i + 1) * 128]

    def put_source(step, x, values):
        for field in range(0, fields, 2):
            place = pl.ds(pl.multiple_of((x + 1) * slab + field * side, 16), 2 * side)
            for part in range(comps):
                pair = [values[field + i, part] for i in (0, 1)]
                columns = slice(part * voxels, (part + 1) * voxels)
                source[step, 1, place, columns] = jnp.concatenate(pair, axis=0).astype(BF16)

    def inside(place_x, place_y):
        return (place_x >= 0) & (place_x < size_x) & (place_y >= 0) & (place_y < size_y)

    def near_copy(step, way):
        move_x, move_y = COMPASS[way]
        if move_y == 0:
            begin, end = (side, 0) if move_x > 0 else (1, side + 1)
            from_ref = source.at[step, 1, pl.ds(begin * slab, slab)]
            to_ref = source.at[step, 1, pl.ds(end * slab, slab)]
        else:
            from_ref = edge_send.at[step, int(move_y > 0)]
            to_ref = edge.at[step, int(move_y > 0)]
            if move_x != 0:
                begin = from_ref.shape[0] - 16 if move_x > 0 else 0
                from_ref, to_ref = from_ref.at[pl.ds(begin, 16)], corner.at[step, way]
        return pltpu.make_async_remote_copy(
            src_ref=from_ref,
            dst_ref=to_ref,
            send_sem=near_send.at[step, way],
            recv_sem=near_receive.at[step, way],
            device_id={"gx": me_x + move_x, "gy": me_y + move_y},
            device_id_type=MESH,
        )

    def band_copy(number, step, way):
        move_x, move_y = COMPASS[way]
        band = bands[number].at[step]
        from_x, to_x = strip(move_x, band.shape[0] - 2)
        from_y, to_y = strip(move_y, band.shape[1] - 2)
        return pltpu.make_async_remote_copy(
            src_ref=band.at[from_x, from_y],
            dst_ref=band.at[to_x, to_y],
            send_sem=band_send.at[number, step, way],
            recv_sem=band_receive.at[number, step, way],
            device_id={"gx": me_x + move_x, "gy": me_y + move_y},
            device_id_type=MESH,
        )

    def near_copies(step):
        return [functools.partial(near_copy, step)]

    def band_copies(step):
        return [functools.partial(band_copy, number, step) for number in range(inner)]

    def start_copies(copies):
        for way, (move_x, move_y) in enumerate(COMPASS):

            @pl.when(inside(me_x + move_x, me_y + move_y))
            def _(way=way):
                for copy in copies:
                    copy(way).start()

    def finish_copies(copies):
        for way, (move_x, move_y) in enumerate(COMPASS):

            @pl.when(inside(me_x + move_x, me_y + move_y))
            def _(way=way):
                for copy in copies:
                    copy(way).wait_send()

            @pl.when(inside(me_x - move_x, me_y - move_y))
            def _(way=way):
                for copy in copies:
                    copy(way).wait_recv()

    def cut_edges(step):
        for i, y in enumerate((0, side - 1)):
            for part in range(width // 128):
                line = product_of[part, pl.ds(y, side * fields, stride=side), :]
                edge_send[step, i, :, part * 128 : (part + 1) * 128] = line.astype(BF16)

    def upward(step):
        own = source[step, 1, slab : slab + rows]
        skeleton[0:rows, 0:rank] = product(own, basis[...], 0)
        parents = []
        for x in range(0, side, 2):
            for y in range(0, side, 2):
                four = [
                    skeleton[pl.ds((x + c) * slab + y + e, 8, stride=side), :][:, :rank]
                    for c, e in CHILDREN
                ]
                parents.append(jnp.concatenate(four, axis=1))
        span = side
        for depth in range(inner):
            span //= 2
            for i, parent in enumerate(parents):
                bands[depth][step, 1 + i // span, 1 + i % span] = parent
            level = times(jnp.concatenate(parents, axis=0), lift_high[depth], lift_low[depth])
            if depth < inner - 1:
                parents = group(level, span, span)
        mine[step] = level
        gathered[step, me] = level

    def gather_of(step):
        return mine.at[step], gathered.at[step], gather_send.at[step], gather_receive.at[step]

    table = near_lookup()

    def near_term(step, a, b, columns):
        slot, flipped = table[(a, b)]
        piece = source[step, 1 + b, (1 + a) * slab : (1 + a) * slab + rows]
        if flipped:
            return product(piece, near[slot, columns, :], 0)
        return product(piece, near[slot, :, columns])

    def widen_edges(step):
        for i in (0, 1):
            edge_wide[i] = edge[step, i].astype(F32)
        for way, (move_x, move_y) in enumerate(COMPASS):
            if move_x != 0 and move_y != 0:
                corner_wide[way] = corner[step, way].astype(F32)

    pieces = chunk // 128
    row_of = lax.broadcasted_iota(jnp.int32, (side, chunk), 0)

    def shift_columns(step, b, index, columns):
        last = side - 1 if b > 0 else 0
        for x in range(-1, side + 1):
            shifted = []
            if x in (-1, side):
                place = slice((x + 1) * slab, (x + 2) * slab)
                own = source[step, 1, place, columns].astype(F32)
                way = COMPASS.index((1 if x < 0 else -1, -b))
                begin = 16 - fields if x < 0 else 0
            else:
                lines = slice(x * slab, (x + 1) * slab)
                own = [product_of[index * pieces + i, lines] for i in range(pieces)]
                own = jnp.concatenate(own, axis=1)
            for field in range(fields):
                value = pltpu.roll(
                    own[field * side : (field + 1) * side], side - 1 if b > 0 else 1, 0
                )
                if x in (-1, side):
                    beyond = corner_wide[way, begin + field : begin + field + 1, columns]
                else:
                    i = x * fields + field
                    beyond = edge_wide[int(b < 0), i : i + 1, columns]
                beyond = jnp.broadcast_to(beyond, value.shape)
                shifted.append(jnp.where(row_of == last, beyond, value))
            for field in range(0, fields, 2):
                begin_row = (x + 1) * slab + field * side
                source[step, 1 + b, begin_row : begin_row + 2 * side, columns] = jnp.concatenate(
                    shifted[field : field + 2], axis=0
                ).astype(BF16)

    def over_columns(work):
        def one(index, carry):
            work(index, pl.ds(pl.multiple_of(index * chunk, chunk), chunk))
            return carry

        lax.fori_loop(0, width // chunk, one, 0)

    def couple(depth, window):
        value = None
        for i, (a, b) in enumerate(HALF_RING):
            for sign in (1, -1):
                term = times(
                    window(sign * a, sign * b),
                    far[depth, i, 0],
                    far[depth, i, 1],
                    1 if sign > 0 else 0,
                )
                value = term if value is None else value + term
        return value

    def near_and_far(step):
        finish_copies(near_copies(step))
        widen_edges(step)

        def straight(index, columns):
            value = near_term(step, 0, 0, columns)
            for a in (-1, 1):
                value = value + near_term(step, a, 0, columns)
            total[:, columns] = value
            shift_columns(step, -1, index, columns)
            shift_columns(step, 1, index, columns)

        over_columns(straight)

        def sideways(index, columns):
            value = total[:, columns]
            for a in (-1, 0, 1):
                for b in (-1, 1):
                    value = value + near_term(step, a, b, columns)
            total[:, columns] = value

        over_columns(sideways)

        finish_copies(band_copies(step))
        here = []
        span = side
        for depth in range(inner):
            span //= 2
            here.append(
                couple(
                    depth,
                    lambda a, b: bands[depth][
                        step, 1 + a : 1 + a + span, 1 + b : 1 + b + span
                    ].reshape(span * span * 8, 4 * rank),
                )
            )
        finish_gather(*gather_of(step))
        across, along = size_x, size_y
        boxes = gathered[step].reshape(devices * 8, rank)
        for up in range(coarse):
            parents = group(boxes, across, along)
            across, along = across // 2, along // 2
            for i, parent in enumerate(parents):
                tops[up][1 + i // along, 1 + i % along] = parent
            if up < coarse - 1:
                boxes = times(
                    jnp.concatenate(parents, axis=0), lift_high[inner + up], lift_low[inner + up]
                )
        down = None
        for up in range(coarse - 1, -1, -1):
            near_x, near_y = me_x >> up + 1, me_y >> up + 1
            value = couple(
                inner + up, lambda a, b: tops[up][near_x + (1 + a), near_y + (1 + b)]
            )
            if down is not None:
                value = value + times(down, lift_high[inner + up], lift_low[inner + up], 0)
            child = 2 * (me_x >> up & 1) + (me_y >> up & 1)
            down = jnp.zeros((8, rank), F32)
            for i in range(4):
                down = jnp.where(child == i, value[:, i * rank : (i + 1) * rank], down)
        span = 1
        for depth in range(inner - 1, -1, -1):
            value = here[depth] + times(down, lift_high[depth], lift_low[depth], 0)
            if depth > 0:
                down = ungroup(value, span, span)
            span *= 2
        for x in range(side):
            for y in range(side):
                place = pl.ds(x * slab + y, fields, stride=side)
                box = child_of(value, x, y, side // 2)
                skeleton[place, :] = jnp.concatenate([box, box], axis=1)[:fields]
        down = skeleton[0:rows, 0:rank]
        high = down.astype(BF16).astype(F32)
        both = jnp.concatenate([high, down - high], axis=1).astype(BF16)
        total[...] = total[...] + product(both, basis_twice[...])

    for i in (0, 1, 2):
        loads[i].wait()
    skeleton[rows:, :] = jnp.zeros((skeleton.shape[0] - rows, skeleton.shape[1]), F32)
    diagonal = lax.broadcasted_iota(jnp.int32, (side, side), 0) == lax.broadcasted_iota(
        jnp.int32, (side, side), 1
    )

    def begin_first(x, add):
        line = jnp.broadcast_to(occupied[pl.ds(x, 1), :].astype(F32), (side, side))
        column = jnp.sum(jnp.where(diagonal, line, 0.0), axis=1, keepdims=True)
        wide = column * contrast[x]
        weight[x] = wide
        values = {}
        for field, part, place, columns in tiles(x):
            value = rhs[x, field, part]
            add(0, field, value * value)
            values[field, part] = wide * value
            put_product(part, place, values[field, part])
        put_source(0, x, values)

    put_sums(0, sweep(1, begin_first))
    cut_edges(0)
    loads[4].wait()
    loads[5].wait()
    for depth in range(levels - 1):
        lift_high[depth], lift_low[depth] = halves(lifts[depth])
    basis_twice[0:rank] = basis[...]
    basis_twice[rank:] = basis[...]
    upward(0)

    pl.semaphore_wait(barrier, devices - 1)
    start_copies(near_copies(0))
    start_gather(*gather_of(0))
    start_copies(band_copies(0))
    start_gather(*sums_of(0))
    loads[6].wait()

    def build(depth, carry):
        far_level(depth, coupling, far)
        return carry

    lax.fori_loop(0, levels, build, 0)
    loads[3].wait()
    near_and_far(0)

    (square_rhs,) = finish_sums(0, 1)
    beta = jnp.sqrt(square_rhs + EPSILON)
    inverse = 1.0 / beta
    norm_first = square_rhs / (square_rhs + EPSILON)

    by_beta = spread(inverse)

    def begin_second(x, add):
        wide = weight[x] * SHRINK
        values = {}
        for field, part, place, columns in tiles(x):
            value = total[place, columns] * by_beta[field]
            image[place, columns] = value
            add(0, field, rhs[x, field, part] * by_beta[field] * value)
            add(1, field, value * value)
            values[field, part] = wide * value
            put_product(part, place, values[field, part])
        put_source(1, x, values)

    sums = sweep(2, begin_second)
    cut_edges(1)
    start_copies(near_copies(1))
    put_sums(1, sums)
    start_gather(*sums_of(1))
    upward(1)
    start_copies(band_copies(1))
    start_gather(*gather_of(1))
    near_and_far(1)

    along, square = finish_sums(1, 2)
    h11 = norm_first + along
    excess = h11 - 1.0
    square = square - 2.0 * excess * along + excess * excess * norm_first
    h21 = jnp.sqrt(square + EPSILON)
    inverse_second = 1.0 / h21
    norm_second = square / (square + EPSILON)
    cross = (along - excess * norm_first) * inverse_second
    grow, back = inverse_second * (1.0 / SHRINK), -excess * inverse_second

    of_second, by_excess, by_grow = spread(inverse_second), spread(excess), spread(grow)
    by_back = spread(back)

    def moved(x, field, part, place, columns):
        held = image[place, columns]
        return total[place, columns] * by_grow[field] + held * by_back[field]

    def second_sums(x, add):
        for field, part, place, columns in tiles(x):
            first = rhs[x, field, part] * by_beta[field]
            second = (image[place, columns] - by_excess[field] * first) * of_second[field]
            value = moved(x, field, part, place, columns)
            add(0, field, first * value)
            add(1, field, second * value)
            add(2, field, value * value)

    put_sums(2, sweep(3, second_sums))
    start_gather(*sums_of(2))
    on_first, on_second, square = finish_sums(2, 3)
    h12 = cross + on_first
    h22 = norm_second + on_second
    over = h22 - 1.0
    square = (
        square
        + h12 * h12 * norm_first
        + over * over * norm_second
        - 2.0 * h12 * on_first
        - 2.0 * over * on_second
        + 2.0 * h12 * over * cross
    )
    h32 = jnp.sqrt(square + EPSILON)
    inverse_third = 1.0 / h32
    of_total = spread(grow * inverse_third)
    of_image = spread((back - over * inverse_second) * inverse_third)
    of_rhs = spread((over * excess * inverse_second - h12) * inverse_third * inverse)

    def out_copy(x):
        return pltpu.make_async_copy(rhs.at[x], third.at[x], unload.at[x])

    def set_third(x, carry):
        for field, part, place, columns in tiles(x):
            rhs[x, field, part] = (
                total[place, columns] * of_total[field]
                + image[place, columns] * of_image[field]
                + rhs[x, field, part] * of_rhs[field]
            )
        out_copy(x).start()
        return carry

    lax.fori_loop(0, side, set_third, 0)
    tile = jnp.zeros((8, 128), F32)
    for i, column in enumerate([beta, h11, h21, h12, h22, h32]):
        tile = jnp.where(lane == i, column, tile)
    hess[...] = tile
    for x in range(side):
        out_copy(x).wait()


def krylov(rhs, contrast, occupied, near, basis, lifts, coupling, count, size_x, size_y):
    side, fields, comps, _, voxels = rhs.shape
    rank, width = basis.shape
    inner = side.bit_length() - 1
    levels = coupling.shape[0]
    coarse = levels - inner
    devices = size_x * size_y
    slab = fields * side
    rows = side * slab
    ways = len(COMPASS)
    arguments = (rhs, contrast, occupied, near, basis, lifts, coupling)
    scratch = [pltpu.VMEM(value.shape, value.dtype) for value in arguments]
    scratch += [
        pltpu.VMEM((levels, len(HALF_RING), 2, 4 * rank, 4 * rank), BF16),
        pltpu.VMEM((levels - 1, 4 * rank, rank), BF16),
        pltpu.VMEM((levels - 1, 4 * rank, rank), BF16),
        pltpu.VMEM((2 * rank, width), BF16),
        pltpu.VMEM(contrast.shape, F32),
        pltpu.VMEM((width // 128, rows, 128), F32),
        pltpu.VMEM((2, 3, rows + 2 * slab, width), BF16),
        pltpu.VMEM((rows, width), F32),
        pltpu.VMEM((rows, width), F32),
        pltpu.VMEM((rows + 2 * side, 128), F32),
        pltpu.VMEM((2, 2, side * fields, width), BF16),
        pltpu.VMEM((2, 2, side * fields, width), BF16),
        pltpu.VMEM((2, ways, 16, width), BF16),
        pltpu.VMEM((2, side * fields, width), F32),
        pltpu.VMEM((ways, 16, width), F32),
    ]
    for depth in range(inner):
        span = (side >> depth + 1) + 2
        scratch.append(pltpu.VMEM((2, span, span, 8, 4 * rank), F32))
    for up in range(coarse):
        grid = ((size_x >> up + 1) + 2, (size_y >> up + 1) + 2)
        scratch.append(pltpu.VMEM(grid + (8, 4 * rank), F32))
    scratch += [
        pltpu.VMEM((2, 8, rank), F32),
        pltpu.VMEM((2, devices, 8, rank), F32),
        pltpu.VMEM((3, 1, 128), F32),
        pltpu.VMEM((3, devices, 1, 128), F32),
        pltpu.SemaphoreType.DMA((2, ways)),
        pltpu.SemaphoreType.DMA((2, ways)),
        pltpu.SemaphoreType.DMA((inner, 2, ways)),
        pltpu.SemaphoreType.DMA((inner, 2, ways)),
        pltpu.SemaphoreType.DMA((2, devices)),
        pltpu.SemaphoreType.DMA((2, devices)),
        pltpu.SemaphoreType.DMA((3, devices)),
        pltpu.SemaphoreType.DMA((3, devices)),
        pltpu.SemaphoreType.DMA((len(arguments),)),
        pltpu.SemaphoreType.DMA((side,)),
    ]
    anywhere = pl.BlockSpec(memory_space=pl.ANY)
    return pl.pallas_call(
        functools.partial(krylov_kernel, size_x, size_y, inner, count),
        in_specs=[anywhere] * len(arguments),
        out_specs=[anywhere, pl.BlockSpec(memory_space=pltpu.VMEM)],
        out_shape=[
            jax.ShapeDtypeStruct(rhs.shape, F32),
            jax.ShapeDtypeStruct((8, 128), F32),
        ],
        scratch_shapes=scratch,
        compiler_params=pltpu.CompilerParams(collective_id=0, has_side_effects=True),
    )(*arguments)


def body(rhs, contrast, occupied, near, basis, transfer, coupling):
    side, _, fields, parts, voxels = rhs.shape
    rank = basis.shape[1]
    devices_x = lax.axis_size("gx")
    devices_y = lax.axis_size("gy")
    count = float(side * side * devices_x * devices_y * parts * voxels)
    lifts = transfer.reshape(transfer.shape[0], 4 * rank, rank)
    third, hess = krylov(
        rhs.transpose(0, 2, 3, 1, 4),
        contrast,
        occupied,
        near,
        basis.T,
        lifts,
        coupling,
        count,
        devices_x,
        devices_y,
    )
    return (third.transpose(0, 3, 1, 2, 4), hess[:fields, :6])


def solution(mesh):
    placed = (
        P("gx", "gy", None, None, None),
        P("gx", "gy", None),
        P("gx", "gy"),
        P(),
        P(),
        P(),
        P(),
    )
    return jax.shard_map(
        body,
        mesh=mesh,
        in_specs=placed,
        out_specs=(P("gx", "gy", None, None, None), P()),
        check_vma=False,
    )
```

time: 77.7 us -> 60.5 us (0.78)
  Pallas kernels: 70.1 us -> 56.7 us
  local copies, waits for them, and re-layouts: 5.06 us -> 2.96 us
  other arithmetic: 1.6 us -> 0 us
    pallas_call x1, Pallas kernels: 70.1 us -> 56.7 us  [krylov(): pl.pallas_call(functools.partial(krylov_kernel, size_x, size_y, inner, co...]
    reshape x1 -> x0, local copies, waits for them, and re-layouts: 2.42 us -> none  [body(): return (third[:, :, :fields].reshape(shape), hess[:fields, :6])]
    unnamed x4, local copies, waits for them, and re-layouts: 1.97 us -> 2.96 us
    mul x1 -> x0, other arithmetic: 0.91 us -> none  [body(): weight = occupied.astype(jnp.float32)[:, :, None] * contrast]
where the time goes in v1:
time: 60.5 us; the launch traced here: 60.3 us
  Pallas kernels  56.7 us (94%)
  local copies, waits for them, and re-layouts  2.96 us (5%)
  between operations  0.65 us (1%)
    pallas_call x1, Pallas kernels, krylov(): pl.pallas_call(functools.partial(krylov_kernel, size_x, size_y, inner, co...  56.7 us
    unnamed x4, local copies, waits for them, and re-layouts  2.96 us

profile of v1, /device:TPU:0, one launch (start us, length us, event | category | flops | bytes accessed | tf_op | source)
XLA Modules:
  0.0 60.3 jit_solution(8160683344121139977)
XLA Ops:
  0.6 56.7 %shard_map.86 = (f32[8,6,3,8,256]{4,3,2,1,0:T(8,128)}, f32[8,128]{1,0:T(8,128)}) custom-call(f32[8,6,3,8,256]{4,3,2,1,0:T(8,128)} %bitcast.5, f32[8,8,256]{2,1,0:T(8,128)} %refs_1_.1, s32[8,8]{1,0:T(8,128)} %refs_2_.1, bf16[5,768,768]{2,1,0:T(8,128)(2,1)} %refs_3_.1, bf16[64,768]{1,0:T(8,128)(2,1)} %bitcast.8, f32[4,256,64]{2,1,0:T(8,128)} %bitcast.7, ...), custom_call_target="tpu_custom_call" | custom-call | tf_op jit(solution)/shard_map/pallas_call | solution.py:723
  57.4 0.0 copy-start
  57.4 2.4 %copy.11 = f32[8,8,6,3,256]{4,1,3,2,0:T(8,128)} copy(f32[8,8,6,3,256]{4,1,3,2,0:T(8,128)} %bitcast.6) | data formatting | bytes 2359296
  59.7 0.0 copy-done
  59.7 0.6 copy.12
Async XLA Ops:
  57.4 2.4 %copy-start = (f32[8,128]{1,0:T(8,128)S(1)}, f32[8,128]{1,0:T(8,128)}, u32[]{:S(2)}) copy-start(f32[8,128]{1,0:T(8,128)} %get-tuple-element.5) | copy-start | bytes 12292

commit v2 on v1

--- a/solution.py
+++ b/solution.py
@@ -135,12 +135,12 @@
 
 
 def krylov_kernel(size_x, size_y, inner, count, *refs):
-    arguments, (third, hess), scratch = refs[:7], refs[7:9], refs[9:]
+    arguments, (image_out, total_out, numbers), scratch = refs[:7], refs[7:10], refs[10:]
     rhs, contrast, occupied, near, basis, lifts, coupling = scratch[:7]
     far, lift_high, lift_low, basis_twice, weight, product_of, source = scratch[7:14]
-    image, total, skeleton, edge_send, edge, corner, edge_wide, corner_wide = scratch[14:22]
-    bands = scratch[22 : 22 + inner]
-    rest = scratch[22 + inner :]
+    image, total, skeleton, edge_send, edge, corner, beyond = scratch[14:21]
+    bands = scratch[21 : 21 + inner]
+    rest = scratch[21 + inner :]
     levels = coupling.shape[0]
     coarse = levels - inner
     tops = rest[:coarse]
@@ -271,11 +271,16 @@
         for field in range(fields):
             place = pl.ds(pl.multiple_of(x * slab + field * side, 8), side)
             for part in range(comps):
-                yield field, part, place, slice(part * voxels, (part + 1) * voxels)
-
-    def put_product(part, place, value):
-        for i in range(voxels // 128):
-            product_of[part * (voxels // 128) + i, place] = value[:, i * 128 : (i + 1) * 128]
+                yield field, part, place
+
+    def put(target, begin, place, value):
+        for i in range(value.shape[1] // 128):
+            target[begin + i, place] = value[:, i * 128 : (i + 1) * 128]
+
+    def get(target, begin, place, amount):
+        return jnp.concatenate([target[begin + i, place] for i in range(amount)], axis=1)
+
+    splits = voxels // 128
 
     def put_source(step, x, values):
         for field in range(0, fields, 2):
@@ -337,8 +342,10 @@
                 for copy in copies:
                     copy(way).start()
 
-    def finish_copies(copies):
+    def finish_copies(copies, wanted=lambda move_y: True):
         for way, (move_x, move_y) in enumerate(COMPASS):
+            if not wanted(move_y):
+                continue
 
             @pl.when(inside(me_x + move_x, me_y + move_y))
             def _(way=way):
@@ -384,51 +391,29 @@
     table = near_lookup()
 
     def near_term(step, a, b, columns):
+        piece = source[step, 1 + b, (1 + a) * slab : (1 + a) * slab + rows]
+        return near_product(a, b, piece, columns)
+
+    def near_product(a, b, piece, columns):
         slot, flipped = table[(a, b)]
-        piece = source[step, 1 + b, (1 + a) * slab : (1 + a) * slab + rows]
         if flipped:
             return product(piece, near[slot, columns, :], 0)
         return product(piece, near[slot, :, columns])
 
-    def widen_edges(step):
-        for i in (0, 1):
-            edge_wide[i] = edge[step, i].astype(F32)
-        for way, (move_x, move_y) in enumerate(COMPASS):
-            if move_x != 0 and move_y != 0:
-                corner_wide[way] = corner[step, way].astype(F32)
-
     pieces = chunk // 128
     row_of = lax.broadcasted_iota(jnp.int32, (side, chunk), 0)
 
-    def shift_columns(step, b, index, columns):
-        last = side - 1 if b > 0 else 0
-        for x in range(-1, side + 1):
-            shifted = []
-            if x in (-1, side):
-                place = slice((x + 1) * slab, (x + 2) * slab)
-                own = source[step, 1, place, columns].astype(F32)
-                way = COMPASS.index((1 if x < 0 else -1, -b))
-                begin = 16 - fields if x < 0 else 0
-            else:
-                lines = slice(x * slab, (x + 1) * slab)
-                own = [product_of[index * pieces + i, lines] for i in range(pieces)]
-                own = jnp.concatenate(own, axis=1)
-            for field in range(fields):
-                value = pltpu.roll(
-                    own[field * side : (field + 1) * side], side - 1 if b > 0 else 1, 0
-                )
-                if x in (-1, side):
-                    beyond = corner_wide[way, begin + field : begin + field + 1, columns]
-                else:
-                    i = x * fields + field
-                    beyond = edge_wide[int(b < 0), i : i + 1, columns]
-                beyond = jnp.broadcast_to(beyond, value.shape)
-                shifted.append(jnp.where(row_of == last, beyond, value))
-            for field in range(0, fields, 2):
-                begin_row = (x + 1) * slab + field * side
-                source[step, 1 + b, begin_row : begin_row + 2 * side, columns] = jnp.concatenate(
-                    shifted[field : field + 2], axis=0
-                ).astype(BF16)
+    def shift_rows(step, b, x, own, columns):
+        shifted = []
+        for field in range(fields):
+            value = own[field * side : (field + 1) * side]
+            value = pltpu.roll(value, side - 1 if b > 0 else 1, 0)
+            shifted.append(jnp.where(row_of == (side - 1 if b > 0 else 0), 0.0, value))
+        for field in range(0, fields, 2):
+            begin = (x + 1) * slab + field * side
+            source[step, 1 + b, begin : begin + 2 * side, columns] = jnp.concatenate(
+                shifted[field : field + 2], axis=0
+            ).astype(BF16)
 
     def over_columns(work):
         def one(index, carry):
@@ -450,29 +435,64 @@
                 value = term if value is None else value + term
         return value
 
+    def near_local(step):
+        def straight(index, columns):
+            put(total, index * pieces, slice(0, rows), near_term(step, 0, 0, columns))
+            for x in range(side):
+                own = get(product_of, index * pieces, slice(x * slab, (x + 1) * slab), pieces)
+                shift_rows(step, -1, x, own, columns)
+                shift_rows(step, 1, x, own, columns)
+
+        over_columns(straight)
+
+        def level(index, columns):
+            value = get(total, index * pieces, slice(0, rows), pieces)
+            for b in (-1, 1):
+                value = value + near_term(step, 0, b, columns)
+            put(total, index * pieces, slice(0, rows), value)
+
+        over_columns(level)
+
+    def beyond_edges(step):
+        finish_copies(near_copies(step), lambda move_y: move_y != 0)
+        last = fields * (side + 1)
+        for i, b in enumerate((1, -1)):
+            low, high = COMPASS.index((1, -b)), COMPASS.index((-1, -b))
+            beyond[i, 0:fields] = corner[step, low].astype(F32)[16 - fields :]
+            beyond[i, fields:last] = edge[step, i].astype(F32)
+            beyond[i, last : last + fields] = corner[step, high].astype(F32)[:fields]
+
+        def one(index, columns):
+            for i, b in enumerate((1, -1)):
+                value = None
+                for a in (-1, 0, 1):
+                    begin = (1 + a) * fields
+                    piece = beyond[i, begin : begin + fields * side].astype(BF16)
+                    term = near_product(a, b, piece, columns)
+                    value = term if value is None else value + term
+                place = pl.ds(side - 1 if b > 0 else 0, fields * side, stride=side)
+                old = get(total, index * pieces, place, pieces)
+                put(total, index * pieces, place, old + value)
+
+        over_columns(one)
+
     def near_and_far(step):
-        finish_copies(near_copies(step))
-        widen_edges(step)
-
-        def straight(index, columns):
-            value = near_term(step, 0, 0, columns)
+        finish_copies(near_copies(step), lambda move_y: move_y == 0)
+        for x in (-1, side):
+            for begin in range(0, width, chunk):
+                columns = slice(begin, begin + chunk)
+                own = source[step, 1, (x + 1) * slab : (x + 2) * slab, columns].astype(F32)
+                shift_rows(step, -1, x, own, columns)
+                shift_rows(step, 1, x, own, columns)
+
+        def sideways(index, columns):
+            value = get(total, index * pieces, slice(0, rows), pieces)
             for a in (-1, 1):
-                value = value + near_term(step, a, 0, columns)
-            total[:, columns] = value
-            shift_columns(step, -1, index, columns)
-            shift_columns(step, 1, index, columns)
-
-        over_columns(straight)
-
-        def sideways(index, columns):
-            value = total[:, columns]
-            for a in (-1, 0, 1):
-                for b in (-1, 1):
+                for b in (-1, 0, 1):
                     value = value + near_term(step, a, b, columns)
-            total[:, columns] = value
+            put(total, index * pieces, slice(0, rows), value)
 
         over_columns(sideways)
-
         finish_copies(band_copies(step))
         here = []
         span = side
@@ -486,6 +506,7 @@
                     ].reshape(span * span * 8, 4 * rank),
                 )
             )
+        beyond_edges(step)
         finish_gather(*gather_of(step))
         across, along = size_x, size_y
         boxes = gathered[step].reshape(devices * 8, rank)
@@ -524,7 +545,11 @@
         down = skeleton[0:rows, 0:rank]
         high = down.astype(BF16).astype(F32)
         both = jnp.concatenate([high, down - high], axis=1).astype(BF16)
-        total[...] = total[...] + product(both, basis_twice[...])
+        for begin in range(0, width, 256):
+            value = product(both, basis_twice[:, begin : begin + 256])
+            amount = value.shape[1] // 128
+            everywhere = slice(0, rows)
+            put(total, begin // 128, everywhere, get(total, begin // 128, everywhere, amount) + value)
 
     for i in (0, 1, 2):
         loads[i].wait()
@@ -539,11 +564,11 @@
         wide = column * contrast[x]
         weight[x] = wide
         values = {}
-        for field, part, place, columns in tiles(x):
+        for field, part, place in tiles(x):
             value = rhs[x, field, part]
             add(0, field, value * value)
             values[field, part] = wide * value
-            put_product(part, place, values[field, part])
+            put(product_of, part * splits, place, values[field, part])
         put_source(0, x, values)
 
     put_sums(0, sweep(1, begin_first))
@@ -556,10 +581,13 @@
     basis_twice[rank:] = basis[...]
     upward(0)
 
+    loads[3].wait()
+    near_local(0)
+
     pl.semaphore_wait(barrier, devices - 1)
     start_copies(near_copies(0))
+    start_copies(band_copies(0))
     start_gather(*gather_of(0))
-    start_copies(band_copies(0))
     start_gather(*sums_of(0))
     loads[6].wait()
 
@@ -568,7 +596,6 @@
         return carry
 
     lax.fori_loop(0, levels, build, 0)
-    loads[3].wait()
     near_and_far(0)
 
     (square_rhs,) = finish_sums(0, 1)
@@ -581,24 +608,29 @@
     def begin_second(x, add):
         wide = weight[x] * SHRINK
         values = {}
-        for field, part, place, columns in tiles(x):
-            value = total[place, columns] * by_beta[field]
-            image[place, columns] = value
+        for field, part, place in tiles(x):
+            value = get(total, part * splits, place, splits) * by_beta[field]
+            put(image, part * splits, place, value)
             add(0, field, rhs[x, field, part] * by_beta[field] * value)
             add(1, field, value * value)
             values[field, part] = wide * value
-            put_product(part, place, values[field, part])
+            put(product_of, part * splits, place, values[field, part])
         put_source(1, x, values)
 
     sums = sweep(2, begin_second)
     cut_edges(1)
     start_copies(near_copies(1))
-    put_sums(1, sums)
-    start_gather(*sums_of(1))
+    image_copy = pltpu.make_async_copy(image, image_out, unload.at[0])
+    image_copy.start()
     upward(1)
     start_copies(band_copies(1))
     start_gather(*gather_of(1))
+    put_sums(1, sums)
+    start_gather(*sums_of(1))
+    near_local(1)
     near_and_far(1)
+    total_copy = pltpu.make_async_copy(total, total_out, unload.at[1])
+    total_copy.start()
 
     along, square = finish_sums(1, 2)
     h11 = norm_first + along
@@ -613,15 +645,13 @@
     of_second, by_excess, by_grow = spread(inverse_second), spread(excess), spread(grow)
     by_back = spread(back)
 
-    def moved(x, field, part, place, columns):
-        held = image[place, columns]
-        return total[place, columns] * by_grow[field] + held * by_back[field]
-
     def second_sums(x, add):
-        for field, part, place, columns in tiles(x):
+        for field, part, place in tiles(x):
             first = rhs[x, field, part] * by_beta[field]
-            second = (image[place, columns] - by_excess[field] * first) * of_second[field]
-            value = moved(x, field, part, place, columns)
+            held = get(image, part * splits, place, splits)
+            second = (held - by_excess[field] * first) * of_second[field]
+            value = get(total, part * splits, place, splits) * by_grow[field]
+            value = value + held * by_back[field]
             add(0, field, first * value)
             add(1, field, second * value)
             add(2, field, value * value)
@@ -642,30 +672,57 @@
     )
     h32 = jnp.sqrt(square + EPSILON)
     inverse_third = 1.0 / h32
-    of_total = spread(grow * inverse_third)
-    of_image = spread((back - over * inverse_second) * inverse_third)
-    of_rhs = spread((over * excess * inverse_second - h12) * inverse_third * inverse)
-
-    def out_copy(x):
-        return pltpu.make_async_copy(rhs.at[x], third.at[x], unload.at[x])
-
-    def set_third(x, carry):
-        for field, part, place, columns in tiles(x):
-            rhs[x, field, part] = (
-                total[place, columns] * of_total[field]
-                + image[place, columns] * of_image[field]
-                + rhs[x, field, part] * of_rhs[field]
-            )
-        out_copy(x).start()
-        return carry
-
-    lax.fori_loop(0, side, set_third, 0)
+    columns = [beta, h11, h21, h12, h22, h32]
+    columns.append(grow * inverse_third)
+    columns.append((back - over * inverse_second) * inverse_third)
+    columns.append((over * excess * inverse_second - h12) * inverse_third * inverse)
     tile = jnp.zeros((8, 128), F32)
-    for i, column in enumerate([beta, h11, h21, h12, h22, h32]):
+    for i, column in enumerate(columns):
         tile = jnp.where(lane == i, column, tile)
-    hess[...] = tile
-    for x in range(side):
-        out_copy(x).wait()
+    numbers[...] = tile
+    image_copy.wait()
+    total_copy.wait()
+
+
+def combine_kernel(rhs, image, total, numbers, third, hess):
+    deep, fields, comps, side, voxels = rhs.shape
+    splits = voxels // 128
+    hess[...] = numbers[:fields, :6]
+    for field in range(fields):
+        of_total, of_image, of_rhs = [
+            jnp.broadcast_to(numbers[field : field + 1, i : i + 1], (side, 128)) for i in (6, 7, 8)
+        ]
+        for x in range(deep):
+            place = slice((x * fields + field) * side, (x * fields + field + 1) * side)
+            for part in range(comps):
+                for i in range(splits):
+                    at = part * splits + i
+                    lanes = slice(i * 128, (i + 1) * 128)
+                    third[x, field, part, :, lanes] = (
+                        total[at, place] * of_total
+                        + image[at, place] * of_image
+                        + rhs[x, field, part, :, lanes] * of_rhs
+                    )
+
+
+def combine(rhs, image, total, numbers):
+    side, fields, comps, _, voxels = rhs.shape
+    deep = 2 if side % 2 == 0 else 1
+    block = (deep,) + rhs.shape[1:]
+    lines = deep * fields * side
+    whole = lambda shape: pl.BlockSpec(shape, lambda i: (0, 0))
+    slabs = pl.BlockSpec((image.shape[0], lines, 128), lambda i: (0, i, 0))
+    boxes = pl.BlockSpec(block, lambda i: (i, 0, 0, 0, 0))
+    return pl.pallas_call(
+        combine_kernel,
+        grid=(side // deep,),
+        in_specs=[boxes, slabs, slabs, whole(numbers.shape)],
+        out_specs=[boxes, whole((fields, 6))],
+        out_shape=[
+            jax.ShapeDtypeStruct(rhs.shape, F32),
+            jax.ShapeDtypeStruct((fields, 6), F32),
+        ],
+    )(rhs, image, total, numbers)
 
 
 def krylov(rhs, contrast, occupied, near, basis, lifts, coupling, count, size_x, size_y):
@@ -688,14 +745,13 @@
         pltpu.VMEM(contrast.shape, F32),
         pltpu.VMEM((width // 128, rows, 128), F32),
         pltpu.VMEM((2, 3, rows + 2 * slab, width), BF16),
-        pltpu.VMEM((rows, width), F32),
-        pltpu.VMEM((rows, width), F32),
+        pltpu.VMEM((width // 128, rows, 128), F32),
+        pltpu.VMEM((width // 128, rows, 128), F32),
         pltpu.VMEM((rows + 2 * side, 128), F32),
         pltpu.VMEM((2, 2, side * fields, width), BF16),
         pltpu.VMEM((2, 2, side * fields, width), BF16),
         pltpu.VMEM((2, ways, 16, width), BF16),
-        pltpu.VMEM((2, side * fields, width), F32),
-        pltpu.VMEM((ways, 16, width), F32),
+        pltpu.VMEM((2, (side + 3) * fields, width), F32),
     ]
     for depth in range(inner):
         span = (side >> depth + 1) + 2
@@ -717,15 +773,16 @@
         pltpu.SemaphoreType.DMA((3, devices)),
         pltpu.SemaphoreType.DMA((3, devices)),
         pltpu.SemaphoreType.DMA((len(arguments),)),
-        pltpu.SemaphoreType.DMA((side,)),
+        pltpu.SemaphoreType.DMA((2,)),
     ]
     anywhere = pl.BlockSpec(memory_space=pl.ANY)
     return pl.pallas_call(
         functools.partial(krylov_kernel, size_x, size_y, inner, count),
         in_specs=[anywhere] * len(arguments),
-        out_specs=[anywhere, pl.BlockSpec(memory_space=pltpu.VMEM)],
+        out_specs=[anywhere, anywhere, pl.BlockSpec(memory_space=pltpu.VMEM)],
         out_shape=[
-            jax.ShapeDtypeStruct(rhs.shape, F32),
+            jax.ShapeDtypeStruct((width // 128, rows, 128), F32),
+            jax.ShapeDtypeStruct((width // 128, rows, 128), F32),
             jax.ShapeDtypeStruct((8, 128), F32),
         ],
         scratch_shapes=scratch,
@@ -734,14 +791,15 @@
 
 
 def body(rhs, contrast, occupied, near, basis, transfer, coupling):
-    side, _, fields, parts, voxels = rhs.shape
+    side, _, _, parts, voxels = rhs.shape
     rank = basis.shape[1]
     devices_x = lax.axis_size("gx")
     devices_y = lax.axis_size("gy")
     count = float(side * side * devices_x * devices_y * parts * voxels)
     lifts = transfer.reshape(transfer.shape[0], 4 * rank, rank)
-    third, hess = krylov(
-        rhs.transpose(0, 2, 3, 1, 4),
+    flat = rhs.transpose(0, 2, 3, 1, 4)
+    image, total, numbers = krylov(
+        flat,
         contrast,
         occupied,
         near,
@@ -752,7 +810,8 @@
         devices_x,
         devices_y,
     )
-    return (third.transpose(0, 3, 1, 2, 4), hess[:fields, :6])
+    third, hess = combine(flat, image, total, numbers)
+    return (third.transpose(0, 3, 1, 2, 4), hess)
 
 
 def solution(mesh):

time: 60.5 us -> 63.5 us (1.050)
  Pallas kernels: 56.7 us -> 62.7 us
  local copies, waits for them, and re-layouts: 2.96 us -> 0 us
    pallas_call x0 -> x1, Pallas kernels: none -> 4.11 us  [combine(): pl.pallas_call(combine_kernel, grid=(side // deep,), in_specs=[boxes, sla...]
    unnamed x4 -> x0, local copies, waits for them, and re-layouts: 2.96 us -> none
    pallas_call x1, Pallas kernels: 56.7 us -> 58.6 us  [krylov(): pl.pallas_call(functools.partial(krylov_kernel, size_x, size_y, inner, co...]
where the time goes in v2:
time: 63.5 us; the launch traced here: 63.3 us
  Pallas kernels  62.7 us (99%)
  between operations  0.64 us (1%)
    pallas_call x1, Pallas kernels, krylov(): pl.pallas_call(functools.partial(krylov_kernel, size_x, size_y, inner, co...  58.6 us
    pallas_call x1, Pallas kernels, combine(): pl.pallas_call(combine_kernel, grid=(side // deep,), in_specs=[boxes, sla...  4.11 us

profile of v2, /device:TPU:0, one launch (start us, length us, event | category | flops | bytes accessed | tf_op | source)
XLA Modules:
  0.0 63.3 jit_solution(18440400161378175981)
XLA Ops:
  0.6 58.6 %shard_map.86 = (f32[6,384,128]{2,1,0:T(8,128)}, f32[6,384,128]{2,1,0:T(8,128)}, f32[8,128]{1,0:T(8,128)}) custom-call(f32[8,6,3,8,256]{4,3,2,1,0:T(8,128)} %bitcast.4, f32[8,8,256]{2,1,0:T(8,128)} %refs_1_.1, s32[8,8]{1,0:T(8,128)} %refs_2_.1, bf16[5,768,768]{2,1,0:T(8,128)(2,1)} %refs_3_.1, bf16[64,768]{1,0:T(8,128)(2,1)} %bitcast.7, ...), custom_call_target="tpu_custom_call" | custom-call | tf_op jit(solution)/shard_map/pallas_call | solution.py:779
  59.2 4.1 %shard_map.87 = (f32[8,6,3,8,256]{4,3,2,1,0:T(8,128)}, f32[6,6]{1,0:T(8,128)}) custom-call(f32[8,6,3,8,256]{4,3,2,1,0:T(8,128)} %bitcast.5, f32[6,384,128]{2,1,0:T(8,128)} %get-tuple-element.7.image, f32[6,384,128]{2,1,0:T(8,128)} %get-tuple-element.8.total, f32[8,128]{1,0:T(8,128)} %get-tuple-element.9.numbers), custom_call_target="tpu_custom_call" | custom-call | tf_op jit(solution)/shard_map/pallas_call | solution.py:716

commit v3 on v2

--- a/solution.py
+++ b/solution.py
@@ -209,21 +209,23 @@
 
     others(greet)
 
-    def gather_copy(piece, target, sent, received, step, to, slot):
+    def gather_copy(piece, target, sent, received, to, slot):
         return pltpu.make_async_remote_copy(
             src_ref=piece,
             dst_ref=target.at[slot],
-            send_sem=sent.at[step],
-            recv_sem=received.at[step],
+            send_sem=sent,
+            recv_sem=received,
             device_id={"gx": to[0], "gy": to[1]},
             device_id_type=MESH,
         )
 
     def start_gather(*what):
-        others(lambda step, to, before: gather_copy(*what, step, to, me).start())
-
-    def finish_gather(*what):
-        others(lambda step, to, before: gather_copy(*what, step, to, before).wait())
+        others(lambda step, to, before: gather_copy(*what, to, me).start())
+
+    def finish_gather(piece, target, sent, received):
+        bulk = target.at[pl.ds(0, devices - 1)]
+        pltpu.make_async_copy(bulk, bulk, received).wait()
+        pltpu.make_async_copy(bulk, bulk, sent).wait()
 
     def sums_of(number):
         return parts.at[number], slots.at[number], sum_send.at[number], sum_receive.at[number]
@@ -304,7 +306,8 @@
             to_ref = edge.at[step, int(move_y > 0)]
             if move_x != 0:
                 begin = from_ref.shape[0] - 16 if move_x > 0 else 0
-                from_ref, to_ref = from_ref.at[pl.ds(begin, 16)], corner.at[step, way]
+                from_ref, to_ref = to_ref.at[pl.ds(begin, 16)], corner.at[step, way]
+                move_y = 0
         return pltpu.make_async_remote_copy(
             src_ref=from_ref,
             dst_ref=to_ref,
@@ -319,6 +322,8 @@
         band = bands[number].at[step]
         from_x, to_x = strip(move_x, band.shape[0] - 2)
         from_y, to_y = strip(move_y, band.shape[1] - 2)
+        if move_x != 0:
+            from_y = to_y = pl.ds(0, band.shape[1])
         return pltpu.make_async_remote_copy(
             src_ref=band.at[from_x, from_y],
             dst_ref=band.at[to_x, to_y],
@@ -334,18 +339,20 @@
     def band_copies(step):
         return [functools.partial(band_copy, number, step) for number in range(inner)]
 
-    def start_copies(copies):
-        for way, (move_x, move_y) in enumerate(COMPASS):
+    along_x = [(COMPASS.index((move, 0)), move, 0) for move in (-1, 1)]
+    along_y = [(COMPASS.index((0, move)), 0, move) for move in (-1, 1)]
+    corners = [(COMPASS.index((a, b)), a, 0) for a in (-1, 1) for b in (-1, 1)]
+
+    def start_copies(copies, ways):
+        for way, move_x, move_y in ways:
 
             @pl.when(inside(me_x + move_x, me_y + move_y))
             def _(way=way):
                 for copy in copies:
                     copy(way).start()
 
-    def finish_copies(copies, wanted=lambda move_y: True):
-        for way, (move_x, move_y) in enumerate(COMPASS):
-            if not wanted(move_y):
-                continue
+    def finish_copies(copies, ways):
+        for way, move_x, move_y in ways:
 
             @pl.when(inside(me_x + move_x, me_y + move_y))
             def _(way=way):
@@ -454,7 +461,7 @@
         over_columns(level)
 
     def beyond_edges(step):
-        finish_copies(near_copies(step), lambda move_y: move_y != 0)
+        finish_copies(near_copies(step), corners)
         last = fields * (side + 1)
         for i, b in enumerate((1, -1)):
             low, high = COMPASS.index((1, -b)), COMPASS.index((-1, -b))
@@ -477,7 +484,7 @@
         over_columns(one)
 
     def near_and_far(step):
-        finish_copies(near_copies(step), lambda move_y: move_y == 0)
+        finish_copies(near_copies(step), along_x)
         for x in (-1, side):
             for begin in range(0, width, chunk):
                 columns = slice(begin, begin + chunk)
@@ -493,20 +500,8 @@
             put(total, index * pieces, slice(0, rows), value)
 
         over_columns(sideways)
-        finish_copies(band_copies(step))
-        here = []
-        span = side
-        for depth in range(inner):
-            span //= 2
-            here.append(
-                couple(
-                    depth,
-                    lambda a, b: bands[depth][
-                        step, 1 + a : 1 + a + span, 1 + b : 1 + b + span
-                    ].reshape(span * span * 8, 4 * rank),
-                )
-            )
-        beyond_edges(step)
+        finish_copies(band_copies(step), along_y)
+        start_copies(band_copies(step), along_x)
         finish_gather(*gather_of(step))
         across, along = size_x, size_y
         boxes = gathered[step].reshape(devices * 8, rank)
@@ -531,6 +526,21 @@
             down = jnp.zeros((8, rank), F32)
             for i in range(4):
                 down = jnp.where(child == i, value[:, i * rank : (i + 1) * rank], down)
+        finish_copies(near_copies(step), along_y)
+        start_copies(near_copies(step), corners)
+        finish_copies(band_copies(step), along_x)
+        here = []
+        span = side
+        for depth in range(inner):
+            span //= 2
+            here.append(
+                couple(
+                    depth,
+                    lambda a, b: bands[depth][
+                        step, 1 + a : 1 + a + span, 1 + b : 1 + b + span
+                    ].reshape(span * span * 8, 4 * rank),
+                )
+            )
         span = 1
         for depth in range(inner - 1, -1, -1):
             value = here[depth] + times(down, lift_high[depth], lift_low[depth], 0)
@@ -545,6 +555,7 @@
         down = skeleton[0:rows, 0:rank]
         high = down.astype(BF16).astype(F32)
         both = jnp.concatenate([high, down - high], axis=1).astype(BF16)
+        beyond_edges(step)
         for begin in range(0, width, 256):
             value = product(both, basis_twice[:, begin : begin + 256])
             amount = value.shape[1] // 128
@@ -585,9 +596,10 @@
     near_local(0)
 
     pl.semaphore_wait(barrier, devices - 1)
-    start_copies(near_copies(0))
-    start_copies(band_copies(0))
+    start_copies(near_copies(0), along_x)
+    start_copies(band_copies(0), along_y)
     start_gather(*gather_of(0))
+    start_copies(near_copies(0), along_y)
     start_gather(*sums_of(0))
     loads[6].wait()
 
@@ -619,12 +631,13 @@
 
     sums = sweep(2, begin_second)
     cut_edges(1)
-    start_copies(near_copies(1))
+    start_copies(near_copies(1), along_x)
     image_copy = pltpu.make_async_copy(image, image_out, unload.at[0])
     image_copy.start()
     upward(1)
-    start_copies(band_copies(1))
+    start_copies(band_copies(1), along_y)
     start_gather(*gather_of(1))
+    start_copies(near_copies(1), along_y)
     put_sums(1, sums)
     start_gather(*sums_of(1))
     near_local(1)
@@ -684,15 +697,36 @@
     total_copy.wait()
 
 
-def combine_kernel(rhs, image, total, numbers, third, hess):
-    deep, fields, comps, side, voxels = rhs.shape
+def combine_kernel(rhs_far, image_far, total_far, numbers, third_far, hess, *scratch):
+    rhs, image, total, third, load, unload = scratch
+    side, fields, comps, _, voxels = rhs.shape
     splits = voxels // 128
+    slab = fields * side
+
+    def copies(x):
+        lines = pl.ds(x * slab, slab)
+        return [
+            pltpu.make_async_copy(rhs_far.at[x], rhs.at[x], load.at[0, x]),
+            pltpu.make_async_copy(image_far.at[:, lines], image.at[:, lines], load.at[1, x]),
+            pltpu.make_async_copy(total_far.at[:, lines], total.at[:, lines], load.at[2, x]),
+        ]
+
+    def result(x):
+        return pltpu.make_async_copy(third.at[x], third_far.at[x], unload.at[x])
+
+    for x in range(side):
+        for copy in copies(x):
+            copy.start()
     hess[...] = numbers[:fields, :6]
-    for field in range(fields):
-        of_total, of_image, of_rhs = [
-            jnp.broadcast_to(numbers[field : field + 1, i : i + 1], (side, 128)) for i in (6, 7, 8)
-        ]
-        for x in range(deep):
+    by = [
+        [jnp.broadcast_to(numbers[field : field + 1, i : i + 1], (side, 128)) for i in (6, 7, 8)]
+        for field in range(fields)
+    ]
+    for x in range(side):
+        for copy in copies(x):
+            copy.wait()
+        for field in range(fields):
+            of_total, of_image, of_rhs = by[field]
             place = slice((x * fields + field) * side, (x * fields + field + 1) * side)
             for part in range(comps):
                 for i in range(splits):
@@ -703,24 +737,30 @@
                         + image[at, place] * of_image
                         + rhs[x, field, part, :, lanes] * of_rhs
                     )
+        result(x).start()
+    for x in range(side):
+        result(x).wait()
 
 
 def combine(rhs, image, total, numbers):
-    side, fields, comps, _, voxels = rhs.shape
-    deep = 2 if side % 2 == 0 else 1
-    block = (deep,) + rhs.shape[1:]
-    lines = deep * fields * side
-    whole = lambda shape: pl.BlockSpec(shape, lambda i: (0, 0))
-    slabs = pl.BlockSpec((image.shape[0], lines, 128), lambda i: (0, i, 0))
-    boxes = pl.BlockSpec(block, lambda i: (i, 0, 0, 0, 0))
+    side, fields = rhs.shape[:2]
+    anywhere = pl.BlockSpec(memory_space=pl.ANY)
+    here = pl.BlockSpec(memory_space=pltpu.VMEM)
     return pl.pallas_call(
         combine_kernel,
-        grid=(side // deep,),
-        in_specs=[boxes, slabs, slabs, whole(numbers.shape)],
-        out_specs=[boxes, whole((fields, 6))],
+        in_specs=[anywhere, anywhere, anywhere, here],
+        out_specs=[anywhere, here],
         out_shape=[
             jax.ShapeDtypeStruct(rhs.shape, F32),
             jax.ShapeDtypeStruct((fields, 6), F32),
+        ],
+        scratch_shapes=[
+            pltpu.VMEM(rhs.shape, F32),
+            pltpu.VMEM(image.shape, F32),
+            pltpu.VMEM(total.shape, F32),
+            pltpu.VMEM(rhs.shape, F32),
+            pltpu.SemaphoreType.DMA((3, side)),
+            pltpu.SemaphoreType.DMA((side,)),
         ],
     )(rhs, image, total, numbers)
 
@@ -768,10 +808,10 @@
         pltpu.SemaphoreType.DMA((2, ways)),
         pltpu.SemaphoreType.DMA((inner, 2, ways)),
         pltpu.SemaphoreType.DMA((inner, 2, ways)),
-        pltpu.SemaphoreType.DMA((2, devices)),
-        pltpu.SemaphoreType.DMA((2, devices)),
-        pltpu.SemaphoreType.DMA((3, devices)),
-        pltpu.SemaphoreType.DMA((3, devices)),
+        pltpu.SemaphoreType.DMA((2,)),
+        pltpu.SemaphoreType.DMA((2,)),
+        pltpu.SemaphoreType.DMA((3,)),
+        pltpu.SemaphoreType.DMA((3,)),
         pltpu.SemaphoreType.DMA((len(arguments),)),
         pltpu.SemaphoreType.DMA((2,)),
     ]

time: 63.5 us -> 53.8 us (0.85)
  Pallas kernels: 62.7 us -> 53 us
    pallas_call x1, Pallas kernels: 58.6 us -> 48.7 us  [krylov(): pl.pallas_call(functools.partial(krylov_kernel, size_x, size_y, inner, co...]
where the time goes in v3:
time: 53.8 us; the launch traced here: 53.7 us
  Pallas kernels  53 us (99%)
  between operations  0.64 us (1%)
    pallas_call x1, Pallas kernels, krylov(): pl.pallas_call(functools.partial(krylov_kernel, size_x, size_y, inner, co...  48.7 us
    pallas_call x1, Pallas kernels, combine(): pl.pallas_call(combine_kernel, in_specs=[anywhere, anywhere, anywhere, he...  4.35 us

profile of v3, /device:TPU:0, one launch (start us, length us, event | category | flops | bytes accessed | tf_op | source)
XLA Modules:
  0.0 53.7 jit_solution(4864001994910436154)
XLA Ops:
  0.6 48.7 %shard_map.86 = (f32[6,384,128]{2,1,0:T(8,128)}, f32[6,384,128]{2,1,0:T(8,128)}, f32[8,128]{1,0:T(8,128)}) custom-call(f32[8,6,3,8,256]{4,3,2,1,0:T(8,128)} %bitcast.4, f32[8,8,256]{2,1,0:T(8,128)} %refs_1_.1, s32[8,8]{1,0:T(8,128)} %refs_2_.1, bf16[5,768,768]{2,1,0:T(8,128)(2,1)} %refs_3_.1, bf16[64,768]{1,0:T(8,128)(2,1)} %bitcast.7, ...), custom_call_target="tpu_custom_call" | custom-call | tf_op jit(solution)/shard_map/pallas_call | solution.py:819
  49.3 4.4 %shard_map.87 = (f32[8,6,3,8,256]{4,3,2,1,0:T(8,128)}, f32[6,6]{1,0:T(8,128)}) custom-call(f32[8,6,3,8,256]{4,3,2,1,0:T(8,128)} %bitcast.5, f32[6,384,128]{2,1,0:T(8,128)} %get-tuple-element.7.image_far, f32[6,384,128]{2,1,0:T(8,128)} %get-tuple-element.8.total_far, f32[8,128]{1,0:T(8,128)} %get-tuple-element.9.numbers), custom_call_target="tpu_custom_call" | custom-call | tf_op jit(solution)/shard_map/pallas_call | solution.py:749

commit v4 on v3

--- a/solution.py
+++ b/solution.py
@@ -592,8 +592,13 @@
     basis_twice[rank:] = basis[...]
     upward(0)
 
-    loads[3].wait()
-    near_local(0)
+    loads[6].wait()
+
+    def build(depth, carry):
+        far_level(depth, coupling, far)
+        return carry
+
+    lax.fori_loop(0, levels, build, 0)
 
     pl.semaphore_wait(barrier, devices - 1)
     start_copies(near_copies(0), along_x)
@@ -601,13 +606,9 @@
     start_gather(*gather_of(0))
     start_copies(near_copies(0), along_y)
     start_gather(*sums_of(0))
-    loads[6].wait()
-
-    def build(depth, carry):
-        far_level(depth, coupling, far)
-        return carry
-
-    lax.fori_loop(0, levels, build, 0)
+    loads[3].wait()
+    near_local(0)
+
     near_and_far(0)
 
     (square_rhs,) = finish_sums(0, 1)
@@ -697,8 +698,8 @@
     total_copy.wait()
 
 
-def combine_kernel(rhs_far, image_far, total_far, numbers, third_far, hess, *scratch):
-    rhs, image, total, third, load, unload = scratch
+def combine_kernel(rhs_far, image_far, total_far, numbers_far, third_far, hess_far, *scratch):
+    rhs, image, total, numbers, third, hess, load, unload, small = scratch
     side, fields, comps, _, voxels = rhs.shape
     splits = voxels // 128
     slab = fields * side
@@ -714,10 +715,15 @@
     def result(x):
         return pltpu.make_async_copy(third.at[x], third_far.at[x], unload.at[x])
 
+    numbers_copy = pltpu.make_async_copy(numbers_far, numbers, small.at[0])
+    hess_copy = pltpu.make_async_copy(hess, hess_far, small.at[1])
+    numbers_copy.start()
     for x in range(side):
         for copy in copies(x):
             copy.start()
+    numbers_copy.wait()
     hess[...] = numbers[:fields, :6]
+    hess_copy.start()
     by = [
         [jnp.broadcast_to(numbers[field : field + 1, i : i + 1], (side, 128)) for i in (6, 7, 8)]
         for field in range(fields)
@@ -740,16 +746,16 @@
         result(x).start()
     for x in range(side):
         result(x).wait()
+    hess_copy.wait()
 
 
 def combine(rhs, image, total, numbers):
     side, fields = rhs.shape[:2]
     anywhere = pl.BlockSpec(memory_space=pl.ANY)
-    here = pl.BlockSpec(memory_space=pltpu.VMEM)
     return pl.pallas_call(
         combine_kernel,
-        in_specs=[anywhere, anywhere, anywhere, here],
-        out_specs=[anywhere, here],
+        in_specs=[anywhere] * 4,
+        out_specs=[anywhere] * 2,
         out_shape=[
             jax.ShapeDtypeStruct(rhs.shape, F32),
             jax.ShapeDtypeStruct((fields, 6), F32),
@@ -758,9 +764,12 @@
             pltpu.VMEM(rhs.shape, F32),
             pltpu.VMEM(image.shape, F32),
             pltpu.VMEM(total.shape, F32),
+            pltpu.VMEM(numbers.shape, F32),
             pltpu.VMEM(rhs.shape, F32),
+            pltpu.VMEM((fields, 6), F32),
             pltpu.SemaphoreType.DMA((3, side)),
             pltpu.SemaphoreType.DMA((side,)),
+            pltpu.SemaphoreType.DMA((2,)),
         ],
     )(rhs, image, total, numbers)
 

time: 53.8 us -> 50.8 us (0.944)
  Pallas kernels: 53 us -> 50 us
    pallas_call x1, Pallas kernels: 48.7 us -> 46.8 us  [krylov(): pl.pallas_call(functools.partial(krylov_kernel, size_x, size_y, inner, co...]
    pallas_call x1, Pallas kernels: 4.35 us -> 3.27 us  [combine(): pl.pallas_call(combine_kernel, in_specs=[anywhere] * 4, out_specs=[anywhe...]
where the time goes in v4:
time: 50.8 us; the launch traced here: 50.7 us
  Pallas kernels  50 us (98%)
  between operations  0.64 us (1%)
    pallas_call x1, Pallas kernels, krylov(): pl.pallas_call(functools.partial(krylov_kernel, size_x, size_y, inner, co...  46.8 us
    pallas_call x1, Pallas kernels, combine(): pl.pallas_call(combine_kernel, in_specs=[anywhere] * 4, out_specs=[anywhe...  3.27 us

profile of v4, /device:TPU:0, one launch (start us, length us, event | category | flops | bytes accessed | tf_op | source)
XLA Modules:
  0.0 50.7 jit_solution(2716221401942119581)
XLA Ops:
  0.6 46.8 %shard_map.86 = (f32[6,384,128]{2,1,0:T(8,128)}, f32[6,384,128]{2,1,0:T(8,128)}, f32[8,128]{1,0:T(8,128)}) custom-call(f32[8,6,3,8,256]{4,3,2,1,0:T(8,128)} %bitcast.4, f32[8,8,256]{2,1,0:T(8,128)} %refs_1_.1, s32[8,8]{1,0:T(8,128)} %refs_2_.1, bf16[5,768,768]{2,1,0:T(8,128)(2,1)} %refs_3_.1, bf16[64,768]{1,0:T(8,128)(2,1)} %bitcast.7, ...), custom_call_target="tpu_custom_call" | custom-call | tf_op jit(solution)/shard_map/pallas_call | solution.py:828
  47.4 3.3 %shard_map.87 = (f32[8,6,3,8,256]{4,3,2,1,0:T(8,128)}, f32[6,6]{1,0:T(8,128)}) custom-call(f32[8,6,3,8,256]{4,3,2,1,0:T(8,128)} %bitcast.5, f32[6,384,128]{2,1,0:T(8,128)} %get-tuple-element.7.image_far, f32[6,384,128]{2,1,0:T(8,128)} %get-tuple-element.8.total_far, f32[8,128]{1,0:T(8,128)} %get-tuple-element.9.numbers_far), custom_call_target="tpu_custom_call" | custom-call | tf_op jit(solution)/shard_map/pallas_call | solution.py:755
